TPU v7x, 32 devices: a whole 2x2x4 slice. The times are simulated.
32 devices in a mesh: parts: 2 (over y), seq: 4 (over z), heads: 2 (over x), sub: 2 (over core).
Axes of the slice: x: 2, y: 2, z: 4, core: 2. Of those that a mesh axis runs over, the one named last changes fastest.
Arguments:
- queries: bfloat16 [8192, 4096], P(('parts', 'seq', 'sub'), 'heads'), parts along dimension 0, as said below
- keys: bfloat16 [8192, 4096], P(('parts', 'seq', 'sub'), 'heads'), parts along dimension 0, as said below
- values: bfloat16 [8192, 4096], P(('parts', 'seq', 'sub'), 'heads'), parts along dimension 0, may hold values from -6 to 6
- half_width: int32 [32], replicated, may hold values from 128 to 512, as said below
- valid_length: int32 [2], P('parts'), parts along dimension 0, may hold values from 3328 to 4096
- out_weight: bfloat16 [4096, 4096], P('heads', 'sub'), may hold values from -1.5 to 1.5
Outputs:
- projected: bfloat16 [8192, 4096], P(('parts', 'seq', 'sub'), 'heads'), parts along dimension 0
There are 2 independent parts, one for each index of `parts`. A program takes and returns all parts, laid end to end along the dimension named above; an argument that names none is the same for every part. Nothing has to cross between parts.
Inputs may be any that keep to these rules, and one draw needn't show every extreme that they name: queries with 32 heads of 128 entries side by side. keys with 32 heads of 128 entries side by side. `half_width`: some head's half-width is exactly 512.
All inputs are finite; a program needn't handle non-finite values.
Results may differ from a plain program's by a relative error of at most 0.014.
Values may be sent and summed in bfloat16 or wider, within the bound.
A program may use at most 192 MiB of HBM per device.

v0:
```python
import functools
import math

import jax
import jax.numpy as jnp
from jax import lax
from jax.experimental import pallas as pl
from jax.experimental.pallas import tpu as pltpu
from jax.sharding import PartitionSpec as P

HD = 128
STEPS = 4
PARTS = 4
CLOSED = -1e30
FAR = 1 << 20
EXP2_SCALE = math.log2(math.e) / math.sqrt(HD)
MESH = pl.DeviceIdType.MESH


def kernel(
    half_width,
    valid_length,
    q_hbm,
    k_hbm,
    v_hbm,
    w_hbm,
    out_ref,
    qbuf,
    kbuf,
    vbuf,
    wbuf,
    distance,
    attended,
    own_terms,
    x_out,
    x_in,
    local_sem,
    z_send,
    z_recv,
    c_send,
    c_recv,
    w_send,
    w_recv,
    x_send,
    x_recv,
):
    rows, width = qbuf.shape
    heads_here = width // HD
    chunk = rows // STEPS
    span = 2 * rows + chunk
    cols = width // PARTS
    seq = lax.axis_index("seq")
    group = lax.axis_index("heads")
    sub = lax.axis_index("sub")
    has_z = jnp.where(sub == 0, seq > 0, seq < lax.axis_size("seq") - 1)
    chip_peer = {"sub": 1 - sub}
    z_peer = {"seq": seq + 2 * sub - 1, "sub": 1 - sub}
    x_peer = {"heads": 1 - group}
    first = (seq * 2 + sub) * rows
    length_end = valid_length[0]

    barrier = pltpu.get_barrier_semaphore()
    pl.semaphore_signal(barrier, inc=1, device_id=chip_peer, device_id_type=MESH)
    pl.semaphore_signal(barrier, inc=1, device_id=x_peer, device_id_type=MESH)

    @pl.when(has_z)
    def _():
        pl.semaphore_signal(barrier, inc=1, device_id=z_peer, device_id_type=MESH)

    own_rows = pl.ds(rows, rows)
    locals_ = [
        pltpu.make_async_copy(q_hbm, qbuf, local_sem.at[0]),
        pltpu.make_async_copy(k_hbm, kbuf.at[own_rows], local_sem.at[1]),
        pltpu.make_async_copy(v_hbm, vbuf.at[own_rows], local_sem.at[2]),
        pltpu.make_async_copy(w_hbm, wbuf.at[sub], local_sem.at[3]),
    ]
    for copy in locals_[:3]:
        copy.start()
    pl.semaphore_wait(barrier, 2 + has_z.astype(jnp.int32))

    def z_copies(step, sender):
        source = jnp.where(sender == 0, step, STEPS - 1 - step) * chunk
        landing = source + jnp.where(sender == 0, 2 * rows, 0)
        source = pl.ds(pl.multiple_of(source, chunk), chunk)
        landing = pl.ds(pl.multiple_of(landing, chunk), chunk)
        return [
            pltpu.make_async_remote_copy(
                src_ref=hbm.at[source],
                dst_ref=buf.at[landing],
                send_sem=z_send.at[which, step],
                recv_sem=z_recv.at[which, step],
                device_id=z_peer,
                device_id_type=MESH,
            )
            for which, (hbm, buf) in enumerate(((k_hbm, kbuf), (v_hbm, vbuf)))
        ]

    def c_copies(sender):
        landing = pl.ds(pl.multiple_of(jnp.where(sender == 0, 0, 2 * rows), chunk), rows)
        return [
            pltpu.make_async_remote_copy(
                src_ref=hbm,
                dst_ref=buf.at[landing],
                send_sem=c_send.at[which],
                recv_sem=c_recv.at[which],
                device_id=chip_peer,
                device_id_type=MESH,
            )
            for which, (hbm, buf) in enumerate(((k_hbm, kbuf), (v_hbm, vbuf)))
        ]

    def w_copy(sender):
        return pltpu.make_async_remote_copy(
            src_ref=w_hbm,
            dst_ref=wbuf.at[sender],
            send_sem=w_send,
            recv_sem=w_recv,
            device_id=chip_peer,
            device_id_type=MESH,
        )

    def query_rows(step):
        return pl.multiple_of(jnp.where(sub == 0, STEPS - 1 - step, step) * chunk, chunk)

    def x_copy(step, part):
        here = (pl.ds(query_rows(step), chunk), pl.ds(part * cols, cols))
        return pltpu.make_async_remote_copy(
            src_ref=x_out.at[here],
            dst_ref=x_in.at[here],
            send_sem=x_send.at[step, part],
            recv_sem=x_recv.at[step, part],
            device_id=x_peer,
            device_id_type=MESH,
        )

    @pl.when(has_z)
    def _():
        for copy in z_copies(0, sub):
            copy.start()

    for copy in c_copies(sub):
        copy.start()

    @pl.when(has_z)
    def _():
        for step in range(1, STEPS):
            for copy in z_copies(step, sub):
                copy.start()

    w_copy(sub).start()
    locals_[3].start()

    @pl.when(jnp.logical_not(has_z))
    def _():
        edge = pl.ds(pl.multiple_of(jnp.where(sub == 0, 0, 2 * rows), chunk), rows)
        kbuf[edge, :] = jnp.zeros((rows, width), kbuf.dtype)
        vbuf[edge, :] = jnp.zeros((rows, width), vbuf.dtype)

    for copy in locals_[:3]:
        copy.wait()
    for copy in c_copies(1 - sub):
        copy.wait_recv()

    def finish(step):
        for part in range(PARTS):
            x_copy(step, part).wait_recv()
        here = pl.ds(query_rows(step), chunk)
        out_ref[here, :] = (own_terms[here, :] + x_in[here, :].astype(jnp.float32)).astype(
            out_ref.dtype
        )

    def one_step(step, carry):
        row = query_rows(step)
        queries_here = pl.ds(row, chunk)
        keys_here = pl.ds(row, span)

        @pl.when(has_z)
        def _():
            for copy in z_copies(step, 1 - sub):
                copy.wait_recv()

        row_at = lax.broadcasted_iota(jnp.int32, (chunk, span), 0)
        key_at = lax.broadcasted_iota(jnp.int32, (chunk, span), 1)
        key_pos = key_at + (first + row - rows)
        distance[...] = jnp.where(
            (key_pos >= 0) & (key_pos < length_end), jnp.abs(row_at + rows - key_at), FAR
        )
        row_fine = (
            lax.broadcasted_iota(jnp.int32, (chunk, HD), 0) + (first + row)
        ) < length_end

        def one_head(head, carry):
            lanes = pl.ds(pl.multiple_of(head * HD, HD), HD)
            scores = lax.dot_general(
                qbuf[queries_here, lanes],
                kbuf[keys_here, lanes],
                (((1,), (1,)), ((), ())),
                preferred_element_type=jnp.float32,
            )
            scores = jnp.where(
                distance[...] <= half_width[group * heads_here + head], scores, CLOSED
            )
            top = jnp.max(scores, axis=1, keepdims=True)
            weights = jnp.exp2((scores - top) * EXP2_SCALE)
            total = jnp.sum(weights, axis=1, keepdims=True)
            sums = jnp.dot(
                weights.astype(jnp.bfloat16),
                vbuf[keys_here, lanes],
                preferred_element_type=jnp.float32,
            )
            attended[:, lanes] = jnp.where(row_fine, sums / total, 0.0).astype(attended.dtype)
            return carry

        lax.fori_loop(0, heads_here, one_head, 0, unroll=2)

        @pl.when(step == 0)
        def _():
            locals_[3].wait()
            w_copy(1 - sub).wait_recv()

        for part in range(2 * PARTS):
            at = pl.ds((part % PARTS) * cols, cols)
            block = 1 - group if part < PARTS else group
            terms = jnp.dot(
                attended[...], wbuf[block, :, at], preferred_element_type=jnp.float32
            )
            if part < PARTS:
                x_out[queries_here, at] = terms.astype(x_out.dtype)
            else:
                own_terms[queries_here, at] = terms
            if 1 <= part <= PARTS:
                x_copy(step, part - 1).start()

        @pl.when(step > 0)
        def _():
            finish(step - 1)

        return carry

    lax.fori_loop(0, STEPS, one_step, 0)
    finish(STEPS - 1)

    for step in range(STEPS):
        for part in range(PARTS):
            x_copy(step, part).wait_send()
    for copy in c_copies(sub):
        copy.wait_send()
    w_copy(sub).wait_send()

    @pl.when(has_z)
    def _():
        for step in range(STEPS):
            for copy in z_copies(step, sub):
                copy.wait_send()


def local(queries, keys, values, half_width, valid_length, out_weight):
    rows, width = queries.shape
    chunk = rows // STEPS
    bf16 = jnp.bfloat16
    dma = pltpu.SemaphoreType.DMA
    return pl.pallas_call(
        kernel,
        out_shape=jax.ShapeDtypeStruct((rows, width), bf16),
        in_specs=[pl.BlockSpec(memory_space=pltpu.SMEM)] * 2
        + [pl.BlockSpec(memory_space=pl.ANY)] * 4,
        out_specs=pl.BlockSpec(memory_space=pltpu.VMEM),
        scratch_shapes=[
            pltpu.VMEM((rows, width), bf16),
            pltpu.VMEM((3 * rows, width), bf16),
            pltpu.VMEM((3 * rows, width), bf16),
            pltpu.VMEM((2,) + out_weight.shape, bf16),
            pltpu.VMEM((chunk, 2 * rows + chunk), jnp.int32),
            pltpu.VMEM((chunk, width), bf16),
            pltpu.VMEM((rows, width), jnp.float32),
            pltpu.VMEM((rows, width), bf16),
            pltpu.VMEM((rows, width), bf16),
            dma((4,)),
            dma((2, STEPS)),
            dma((2, STEPS)),
            dma((2,)),
            dma((2,)),
            dma,
            dma,
            dma((STEPS, PARTS)),
            dma((STEPS, PARTS)),
        ],
        compiler_params=pltpu.CompilerParams(
            collective_id=0, has_side_effects=True, vmem_limit_bytes=60 << 20
        ),
    )(half_width, valid_length, queries, keys, values, out_weight)


def solution(mesh):
    placed = (
        P(("parts", "seq", "sub"), "heads"),
        P(("parts", "seq", "sub"), "heads"),
        P(("parts", "seq", "sub"), "heads"),
        P(),
        P("parts"),
        P("heads", "sub"),
    )
    return jax.shard_map(
        local,
        mesh=mesh,
        in_specs=placed,
        out_specs=P(("parts", "seq", "sub"), "heads"),
        check_vma=False,
    )
```

profile of v0, /device:TPU:17, one launch (start us, length us, event | category | flops | bytes accessed | tf_op | source)
XLA Modules:
  0.0 79.8 jit_solution(4417135705184703738)
XLA Ops:
  0.7 75.9 %shard_map.64 = bf16[512,2048]{1,0:T(8,128)(2,1)} custom-call(s32[32]{0:T(128)} %half_width.1, s32[1]{0:T(128)S(6)} %copy.8.valid_length, bf16[512,2048]{1,0:T(8,128)(2,1)} %q_hbm.1, bf16[512,2048]{1,0:T(8,128)(2,1)} %k_hbm.1, bf16[512,2048]{1,0:T(8,128)(2,1)} %v_hbm.1, bf16[2048,2048]{1,0:T(8,128)(2,1)} %w_hbm.1), custom_call_target="tpu_custom_call" | custom-call | tf_op jit(solution)/shard_map/pallas_call | solution.py:262
  76.6 3.2 %copy.9 = bf16[512,2048]{1,0:T(8,128)(2,1)} copy(bf16[512,2048]{1,0:T(8,128)(2,1)} %shard_map.64) | data formatting | bytes 4194304
where the time goes:
time: 79.9 us; the launch traced here: 79.8 us
  Pallas kernels  75.9 us (95%)
  local copies, waits for them, and re-layouts  3.16 us (4%)
    pallas_call x1, Pallas kernels, local(): pl.pallas_call(kernel, out_shape=jax.ShapeDtypeStruct((rows, width), bf16...  75.9 us
    unnamed x1, local copies, waits for them, and re-layouts  3.16 us

commit v1 on v0

--- a/solution.py
+++ b/solution.py
@@ -9,7 +9,10 @@
 from jax.sharding import PartitionSpec as P
 
 HD = 128
-STEPS = 4
+LAYERS = (128, 128, 128, 128)
+REACH = 128
+STEPS = len(LAYERS)
+STARTS = tuple(sum(LAYERS[:step]) for step in range(STEPS))
 PARTS = 4
 CLOSED = -1e30
 FAR = 1 << 20
@@ -46,8 +49,7 @@
 ):
     rows, width = qbuf.shape
     heads_here = width // HD
-    chunk = rows // STEPS
-    span = 2 * rows + chunk
+    span = 2 * rows + REACH
     cols = width // PARTS
     seq = lax.axis_index("seq")
     group = lax.axis_index("heads")
@@ -79,10 +81,11 @@
     pl.semaphore_wait(barrier, 2 + has_z.astype(jnp.int32))
 
     def z_copies(step, sender):
-        source = jnp.where(sender == 0, step, STEPS - 1 - step) * chunk
+        start, size = STARTS[step], LAYERS[step]
+        source = jnp.where(sender == 0, start, rows - size - start)
         landing = source + jnp.where(sender == 0, 2 * rows, 0)
-        source = pl.ds(pl.multiple_of(source, chunk), chunk)
-        landing = pl.ds(pl.multiple_of(landing, chunk), chunk)
+        source = pl.ds(pl.multiple_of(source, 32), size)
+        landing = pl.ds(pl.multiple_of(landing, 32), size)
         return [
             pltpu.make_async_remote_copy(
                 src_ref=hbm.at[source],
@@ -96,7 +99,7 @@
         ]
 
     def c_copies(sender):
-        landing = pl.ds(pl.multiple_of(jnp.where(sender == 0, 0, 2 * rows), chunk), rows)
+        landing = pl.ds(pl.multiple_of(jnp.where(sender == 0, 0, 2 * rows), rows), rows)
         return [
             pltpu.make_async_remote_copy(
                 src_ref=hbm,
@@ -120,10 +123,11 @@
         )
 
     def query_rows(step):
-        return pl.multiple_of(jnp.where(sub == 0, STEPS - 1 - step, step) * chunk, chunk)
+        start, size = STARTS[step], LAYERS[step]
+        return pl.multiple_of(jnp.where(sub == 0, rows - size - start, start), 32)
 
     def x_copy(step, part):
-        here = (pl.ds(query_rows(step), chunk), pl.ds(part * cols, cols))
+        here = (pl.ds(query_rows(step), LAYERS[step]), pl.ds(part * cols, cols))
         return pltpu.make_async_remote_copy(
             src_ref=x_out.at[here],
             dst_ref=x_in.at[here],
@@ -152,7 +156,7 @@
 
     @pl.when(jnp.logical_not(has_z))
     def _():
-        edge = pl.ds(pl.multiple_of(jnp.where(sub == 0, 0, 2 * rows), chunk), rows)
+        edge = pl.ds(pl.multiple_of(jnp.where(sub == 0, 0, 2 * rows), rows), rows)
         kbuf[edge, :] = jnp.zeros((rows, width), kbuf.dtype)
         vbuf[edge, :] = jnp.zeros((rows, width), vbuf.dtype)
 
@@ -164,15 +168,17 @@
     def finish(step):
         for part in range(PARTS):
             x_copy(step, part).wait_recv()
-        here = pl.ds(query_rows(step), chunk)
+        here = pl.ds(query_rows(step), LAYERS[step])
         out_ref[here, :] = (own_terms[here, :] + x_in[here, :].astype(jnp.float32)).astype(
             out_ref.dtype
         )
 
-    def one_step(step, carry):
+    def one_step(step):
+        chunk = LAYERS[step]
         row = query_rows(step)
+        lead = jnp.where(sub == 0, 0, REACH - chunk)
         queries_here = pl.ds(row, chunk)
-        keys_here = pl.ds(row, span)
+        keys_here = pl.ds(pl.multiple_of(row - lead, 32), span)
 
         @pl.when(has_z)
         def _():
@@ -181,9 +187,9 @@
 
         row_at = lax.broadcasted_iota(jnp.int32, (chunk, span), 0)
         key_at = lax.broadcasted_iota(jnp.int32, (chunk, span), 1)
-        key_pos = key_at + (first + row - rows)
-        distance[...] = jnp.where(
-            (key_pos >= 0) & (key_pos < length_end), jnp.abs(row_at + rows - key_at), FAR
+        key_pos = key_at + (first + row - lead - rows)
+        distance[:chunk, :] = jnp.where(
+            (key_pos >= 0) & (key_pos < length_end), jnp.abs(row_at + (rows + lead) - key_at), FAR
         )
         row_fine = (
             lax.broadcasted_iota(jnp.int32, (chunk, HD), 0) + (first + row)
@@ -198,7 +204,7 @@
                 preferred_element_type=jnp.float32,
             )
             scores = jnp.where(
-                distance[...] <= half_width[group * heads_here + head], scores, CLOSED
+                distance[:chunk, :] <= half_width[group * heads_here + head], scores, CLOSED
             )
             top = jnp.max(scores, axis=1, keepdims=True)
             weights = jnp.exp2((scores - top) * EXP2_SCALE)
@@ -208,13 +214,12 @@
                 vbuf[keys_here, lanes],
                 preferred_element_type=jnp.float32,
             )
-            attended[:, lanes] = jnp.where(row_fine, sums / total, 0.0).astype(attended.dtype)
+            attended[:chunk, lanes] = jnp.where(row_fine, sums / total, 0.0).astype(attended.dtype)
             return carry
 
-        lax.fori_loop(0, heads_here, one_head, 0, unroll=2)
-
-        @pl.when(step == 0)
-        def _():
+        lax.fori_loop(0, heads_here, one_head, 0, unroll=4)
+
+        if step == 0:
             locals_[3].wait()
             w_copy(1 - sub).wait_recv()
 
@@ -222,7 +227,7 @@
             at = pl.ds((part % PARTS) * cols, cols)
             block = 1 - group if part < PARTS else group
             terms = jnp.dot(
-                attended[...], wbuf[block, :, at], preferred_element_type=jnp.float32
+                attended[:chunk, :], wbuf[block, :, at], preferred_element_type=jnp.float32
             )
             if part < PARTS:
                 x_out[queries_here, at] = terms.astype(x_out.dtype)
@@ -231,13 +236,11 @@
             if 1 <= part <= PARTS:
                 x_copy(step, part - 1).start()
 
-        @pl.when(step > 0)
-        def _():
+        if step > 0:
             finish(step - 1)
 
-        return carry
-
-    lax.fori_loop(0, STEPS, one_step, 0)
+    for step in range(STEPS):
+        one_step(step)
     finish(STEPS - 1)
 
     for step in range(STEPS):
@@ -256,7 +259,6 @@
 
 def local(queries, keys, values, half_width, valid_length, out_weight):
     rows, width = queries.shape
-    chunk = rows // STEPS
     bf16 = jnp.bfloat16
     dma = pltpu.SemaphoreType.DMA
     return pl.pallas_call(
@@ -270,8 +272,8 @@
             pltpu.VMEM((3 * rows, width), bf16),
             pltpu.VMEM((3 * rows, width), bf16),
             pltpu.VMEM((2,) + out_weight.shape, bf16),
-            pltpu.VMEM((chunk, 2 * rows + chunk), jnp.int32),
-            pltpu.VMEM((chunk, width), bf16),
+            pltpu.VMEM((REACH, 2 * rows + REACH), jnp.int32),
+            pltpu.VMEM((REACH, width), bf16),
             pltpu.VMEM((rows, width), jnp.float32),
             pltpu.VMEM((rows, width), bf16),
             pltpu.VMEM((rows, width), bf16),

time: 79.9 us -> 77.9 us (0.975)
  Pallas kernels: 75.9 us -> 73.9 us
    pallas_call x1, Pallas kernels: 75.9 us -> 73.9 us  [local(): pl.pallas_call(kernel, out_shape=jax.ShapeDtypeStruct((rows, width), bf16...]
where the time goes in v1:
time: 77.9 us; the launch traced here: 77.8 us
  Pallas kernels  73.9 us (95%)
  local copies, waits for them, and re-layouts  3.16 us (4%)
    pallas_call x1, Pallas kernels, local(): pl.pallas_call(kernel, out_shape=jax.ShapeDtypeStruct((rows, width), bf16...  73.9 us
    unnamed x1, local copies, waits for them, and re-layouts  3.16 us

profile of v1, /device:TPU:17, one launch (start us, length us, event | category | flops | bytes accessed | tf_op | source)
XLA Modules:
  0.0 77.8 jit_solution(7880831321796001432)
XLA Ops:
  0.7 73.9 %shard_map.64 = bf16[512,2048]{1,0:T(8,128)(2,1)} custom-call(s32[32]{0:T(128)} %half_width.1, s32[1]{0:T(128)S(6)} %copy.8.valid_length, bf16[512,2048]{1,0:T(8,128)(2,1)} %q_hbm.1, bf16[512,2048]{1,0:T(8,128)(2,1)} %k_hbm.1, bf16[512,2048]{1,0:T(8,128)(2,1)} %v_hbm.1, bf16[2048,2048]{1,0:T(8,128)(2,1)} %w_hbm.1), custom_call_target="tpu_custom_call" | custom-call | tf_op jit(solution)/shard_map/pallas_call | solution.py:264
  74.6 3.2 %copy.9 = bf16[512,2048]{1,0:T(8,128)(2,1)} copy(bf16[512,2048]{1,0:T(8,128)(2,1)} %shard_map.64) | data formatting | bytes 4194304
